TPU v7x, 32 devices: a whole 2x2x4 slice. The times are simulated.
32 devices in a mesh: pole: 2 (over x), wide: 8 (over z, y), narrow: 2 (over core).
Axes of the slice: x: 2, y: 2, z: 4, core: 2. Of those that a mesh axis runs over, the one named last changes fastest.
Arguments:
- h_panel: float32 [512, 2048], P(('pole', 'wide', 'narrow')), parts along dimension 0, may hold values from -0.3 to 0.3
- s_panel: float32 [512, 2048], P(('pole', 'wide', 'narrow')), parts along dimension 0, may hold values from -0.3 to 0.3
- col_index: int32 [512], P('pole'), parts along dimension 0, may hold values from 0 to 255, each once
- pattern: int32 [256], P(('pole', 'wide', 'narrow')), parts along dimension 0, may hold values 0 or 1
- dinv: float32 [512, 256], P('pole'), parts along dimension 0, may hold values from -4 to 4, as said below
- ainv_cc: float32 [4096, 8, 2, 128], P(('pole', 'wide'), None, 'narrow'), parts along dimension 0, may hold values from -1 to 1
Outputs:
- ainv_ck: float32 [4096, 256], P(('pole', 'wide'), 'narrow'), parts along dimension 0
- ainv_kk: float32 [512, 256], P(('pole', 'wide'), 'narrow'), parts along dimension 0
There are 2 independent parts, one for each index of `pole`. A program takes and returns all parts, laid end to end along the dimension named above; each array names one. Nothing has to cross between parts.
Inputs may be any that keep to these rules, and one draw needn't show every extreme that they name: `dinv`: diagonal entries between 0.25 and 4, off-diagonal entries at most 4 / sqrt(256) in magnitude.
All inputs are finite; a program needn't handle non-finite values. No bound on the sum of `pattern` on one device may be relied on, other than what follows from the above.
Results may differ from a plain program's by a relative error of at most 0.00011.
Values sent between devices are 32-bit elements; how exact they have to be, the bound alone decides.
No kernel may reach another device: no remote copies, remote signals or barrier semaphores. Data moves between devices by JAX's collectives and lax.ppermute only.
A program may use at most 64 MiB of HBM per device.

v0:
```python
import jax
import jax.numpy as jnp
from jax import lax
from jax.sharding import PartitionSpec as P

POLE_SHIFT = 0.5


def local(h_panel, s_panel, col_index, pattern, dinv, ainv_cc):
    panel_cols = h_panel - POLE_SHIFT * s_panel
    super_width = dinv.shape[0]
    received = lax.all_to_all(
        panel_cols, ("wide", "narrow"), split_axis=1, concat_axis=0, tiled=True
    )
    dinv_rows = jnp.take(dinv, col_index, axis=0)
    factor_panel = lax.dot_general(
        received,
        dinv_rows,
        (((0,), (0,)), ((), ())),
        precision=lax.Precision.HIGHEST,
        preferred_element_type=jnp.float32,
    )
    live_rows = (pattern > 0).astype(jnp.float32)
    factor_panel = (
        factor_panel.reshape(live_rows.shape[0], -1, super_width) * live_rows[:, None, None]
    ).reshape(factor_panel.shape)
    rows_here = ainv_cc.shape[0]
    inverse_flat = ainv_cc.reshape(rows_here, -1)
    partial_value = jnp.dot(
        inverse_flat,
        lax.all_gather(factor_panel, "wide", axis=0, tiled=True),
        precision=lax.Precision.HIGHEST,
        preferred_element_type=jnp.float32,
    )
    ainv_ck = -lax.psum_scatter(partial_value, "narrow", scatter_dimension=1, tiled=True)
    paired = lax.all_gather(factor_panel, "narrow", axis=0, tiled=True)
    corner_term = lax.dot_general(
        paired,
        ainv_ck,
        (((0,), (0,)), ((), ())),
        precision=lax.Precision.HIGHEST,
        preferred_element_type=jnp.float32,
    )
    summed = lax.psum_scatter(corner_term, "wide", scatter_dimension=0, tiled=True)
    half_width = ainv_ck.shape[1]
    rows_corner = summed.shape[0]
    corner = lax.dynamic_slice(
        dinv,
        (lax.axis_index("wide") * rows_corner, lax.axis_index("narrow") * half_width),
        (rows_corner, half_width),
    )
    return (ainv_ck, corner - summed)


def solution(mesh):
    placed = (
        P(("pole", "wide", "narrow"), None),
        P(("pole", "wide", "narrow"), None),
        P("pole"),
        P(("pole", "wide", "narrow")),
        P("pole", None),
        P(("pole", "wide"), None, "narrow", None),
    )
    return jax.shard_map(
        local,
        mesh=mesh,
        in_specs=placed,
        out_specs=(P(("pole", "wide"), "narrow"), P(("pole", "wide"), "narrow")),
        check_vma=False,
    )
```

profile of v0, /device:TPU:0, one launch (start us, length us, event | category | flops | bytes accessed | tf_op | source)
XLA Modules:
  0.0 148.3 jit_solution(7724145951328195672)
XLA Ops:
  7.2 0.0 copy-start
  7.2 1.7 %copy_bitcast_fusion = f32[16,16,128]{2,0,1:T(8,128)} fusion(f32[16,2048]{1,0:T(8,128)} %param.6, f32[16,2048]{1,0:T(8,128)} %param.7), kind=kLoop, calls=%fused_computation.7 | loop fusion | flops 65536 | bytes 393216 | tf_op jit(solution)/shard_map/all_to_all | solution.py:12
  8.9 0.0 copy-start.4
  8.9 7.5 %all-to-all-start = ((f32[16,16,128]{2,0,1:T(8,128)}), f32[16,16,128]{2,0,1:T(8,128)S(1)}, u32[]{:S(2)}, u32[]{:S(2)}) async-start(f32[16,16,128]{2,0,1:T(8,128)} %copy_bitcast_fusion), calls=%async_computation | async-start | bytes 262144 | tf_op jit(solution)/shard_map/all_to_all | solution.py:12
  16.4 0.0 copy-start.5
  16.4 0.0 all-gather.2.cloned.1.call-start
  16.5 0.0 copy-done.4
  16.5 0.6 copy-done.5
  17.1 0.0 copy-done
  17.1 0.0 copy-start.2
  17.1 1.0 gather_fusion
  18.1 6.2 %all-to-all-done = f32[16,16,128]{2,0,1:T(8,128)S(1)} async-done(((f32[16,16,128]{2,0,1:T(8,128)}), f32[16,16,128]{2,0,1:T(8,128)S(1)}, u32[]{:S(2)}, u32[]{:S(2)}) %all-to-all-start) | async-done | bytes 131104 | tf_op jit(solution)/shard_map/all_to_all | solution.py:12
  24.3 0.1 copy.16
  24.4 1.0 convolution_multiply_fusion
  25.4 0.0 all-gather.2.cloned.1.call-update
  25.5 0.0 reduce-scatter.3.cloned.1.call-start
  25.5 38.2 %all-gather.2.cloned.1.call-done = f32[1024,256]{1,0:T(8,128)} async-done(((f32[128,256]{1,0:T(8,128)}), f32[1024,256]{1,0:T(8,128)}) %all-gather.2.cloned.1.call-update) | async-done | bytes 1048592 | tf_op jit(solution)/shard_map/all_gather | solution.py:31
  63.7 0.0 copy-done.2
  63.7 3.8 %convolution_bitcast_fusion = f32[256,256]{0,1:T(8,128)} fusion(f32[1024,256]{1,0:T(8,128)} %all-gather.2.cloned.1.call-done, f32[32,8,8,128]{3,2,1,0:T(8,128)S(1)} %bitcast.28), kind=kOutput, calls=%fused_computation.1 | convolution fusion | flops 805306368 | bytes 2359296 | tf_op jit(solution)/shard_map/dot_general | solution.py:29
  67.5 0.0 copy-start.1
  67.5 0.0 reduce-scatter.3.cloned.1.call-update
  67.5 0.0 reduce-scatter.5.cloned.1.call-start
  67.5 0.8 copy-done.1
  68.4 2.0 %all_gather.7 = f32[256,256]{1,0:T(8,128)S(1)} all-gather(f32[128,256]{1,0:T(8,128)S(1)} %bitcast.27), channel_id=1, replica_groups=mesh['pole'=2,'wide'=8,'narrow'=2] {'narrow'}, dimensions={0}, use_global_device_ids=true | all-gather | bytes 393216 | tf_op jit(solution)/shard_map/all_gather | solution.py:36
  70.4 3.7 %reduce-scatter.3.cloned.1.call-done = f32[256,128]{0,1:T(8,128)} async-done(((f32[256,256]{0,1:T(8,128)}), f32[256,128]{0,1:T(8,128)}) %reduce-scatter.3.cloned.1.call-update) | async-done | bytes 131088 | tf_op jit(solution)/shard_map/reduce_scatter | solution.py:35
  74.1 2.2 %fusion.7 = f32[256,128]{1,0:T(8,128)} fusion(f32[256,256]{1,0:T(8,128)S(1)} %all_gather.7, f32[256,128]{0,1:T(8,128)} %reduce-scatter.3.cloned.1.call-done), kind=kOutput, calls=%fused_computation.17 | convolution fusion | flops 100696064 | bytes 524288 | tf_op jit(solution)/shard_map/dot_general | solution.py:37
  76.3 0.0 copy-start.3
  76.3 0.0 reduce-scatter.5.cloned.1.call-update
  76.3 0.9 copy-done.3
  77.2 0.8 copy.17
  77.9 62.5 %reduce-scatter.5.cloned.1.call-done = f32[32,128]{1,0:T(8,128)} async-done(((f32[256,128]{1,0:T(8,128)}), f32[32,128]{1,0:T(8,128)}) %reduce-scatter.5.cloned.1.call-update) | async-done | bytes 16400 | tf_op jit(solution)/shard_map/reduce_scatter | solution.py:44
  140.4 1.3 dynamic-slice_subtract_fusion
  (5 shorter events, 0.0 us)
Async XLA Ops:
  7.2 9.9 %copy-start = (f32[256,256]{1,0:T(8,128)S(1)}, f32[256,256]{1,0:T(8,128)}, u32[]{:S(2)}) copy-start(f32[256,256]{1,0:T(8,128)} %param.10) | copy-start | bytes 786436
  8.9 7.6 %copy-start.4 = (s32[256]{0:T(256)S(1)}, s32[256]{0:T(256)}, u32[]{:S(2)}) copy-start(s32[256]{0:T(256)} %param.8) | copy-start | bytes 3076
  8.9 15.5 %all-to-all-start = ((f32[16,16,128]{2,0,1:T(8,128)}), f32[16,16,128]{2,0,1:T(8,128)S(1)}, u32[]{:S(2)}, u32[]{:S(2)}) async-start(f32[16,16,128]{2,0,1:T(8,128)} %copy_bitcast_fusion), calls=%async_computation | async-start | bytes 262144 | tf_op jit(solution)/shard_map/all_to_all | solution.py:12
  16.4 0.7 copy-start.5
  16.4 47.2 %all-gather.2.cloned.1.call-start = ((), (), s32[]{:S(2)}) async-start(), calls=%async_computation.3 | async-start | bytes 1179648 | tf_op jit(solution)/shard_map/all_gather | solution.py:31
  17.1 46.6 %copy-start.2 = (f32[256,8,1,128]{3,2,1,0:T(1,128)S(1)}, f32[256,8,1,128]{3,2,1,0:T(1,128)}, u32[]{:S(2)}) copy-start(f32[256,8,1,128]{3,2,1,0:T(1,128)} %param.11) | copy-start | bytes 3145732
  25.5 48.6 %reduce-scatter.3.cloned.1.call-start = ((), (), s32[]{:S(2)}) async-start(), calls=%async_computation.4 | async-start | bytes 393216 | tf_op jit(solution)/shard_map/reduce_scatter | solution.py:35
  67.5 0.9 copy-start.1
  67.5 72.9 %reduce-scatter.5.cloned.1.call-start = ((), (), s32[]{:S(2)}) async-start(), calls=%async_computation.5 | async-start | bytes 147456 | tf_op jit(solution)/shard_map/reduce_scatter | solution.py:44
  76.3 0.9 copy-start.3
Sparse Core Ops, SparseCore 0:
  25.6 38.0 all-gather.1
  67.6 6.4 reduce-scatter.2
  77.4 62.9 reduce-scatter.4
where the time goes:
time: 149 us; the launch traced here: 148 us
  waiting for transfers between devices  111 us (74%)
  between operations  13.8 us (9%)
  starting transfers between devices  7.67 us (5%)
  matrix products  6.98 us (5%)
  local copies, waits for them, and re-layouts  4.11 us (3%)
  other arithmetic  3.04 us (2%)
  blocking collectives  1.98 us (1%)
    reduce_scatter x1, waiting for transfers between devices, local(): lax.psum_scatter(corner_term, 'wide', scatter_dimension=0, tiled=True)  62.5 us
    all_gather x1, waiting for transfers between devices, local(): lax.all_gather(factor_panel, 'wide', axis=0, tiled=True)  38.2 us
    all_to_all x1, starting transfers between devices, local(): lax.all_to_all(panel_cols, ('wide', 'narrow'), split_axis=1, concat_axis=...  7.55 us
    all_to_all x1, waiting for transfers between devices, local(): lax.all_to_all(panel_cols, ('wide', 'narrow'), split_axis=1, concat_axis=...  6.22 us
    dot_general x1, matrix products, local(): jnp.dot(inverse_flat, lax.all_gather(factor_panel, 'wide', axis=0, tiled=...  3.8 us
    reduce_scatter x1, waiting for transfers between devices, local(): lax.psum_scatter(partial_value, 'narrow', scatter_dimension=1, tiled=True)  3.75 us
    unnamed x13, local copies, waits for them, and re-layouts  3.05 us
  transfers between devices with their start and end apart: 4, of which 4 were waited for; matrix products, arithmetic and copies ran while one was open for 1% of the time, Pallas kernels for 0%

commit v1 on v0

--- a/solution.py
+++ b/solution.py
@@ -9,8 +9,14 @@
 def local(h_panel, s_panel, col_index, pattern, dinv, ainv_cc):
     panel_cols = h_panel - POLE_SHIFT * s_panel
     super_width = dinv.shape[0]
-    received = lax.all_to_all(
-        panel_cols, ("wide", "narrow"), split_axis=1, concat_axis=0, tiled=True
+    received = jnp.concatenate(
+        lax.all_to_all(
+            jnp.stack(jnp.split(panel_cols, lax.axis_size(("wide", "narrow")), axis=1)),
+            ("wide", "narrow"),
+            0,
+            0,
+        ),
+        axis=0,
     )
     dinv_rows = jnp.take(dinv, col_index, axis=0)
     factor_panel = lax.dot_general(

time: 149 us -> 158 us (1.060)
  local copies, waits for them, and re-layouts: 4.11 us -> 13.7 us
    unnamed x13 -> x28, local copies, waits for them, and re-layouts: 3.05 us -> 12 us
    all_to_all x1 -> x0, other arithmetic: 1.68 us -> none  [local(): lax.all_to_all(panel_cols, ('wide', 'narrow'), split_axis=1, concat_axis=...]
where the time goes in v1:
time: 158 us; the launch traced here: 157 us
  waiting for transfers between devices  111 us (70%)
  between operations  13.8 us (9%)
  local copies, waits for them, and re-layouts  13.7 us (9%)
  starting transfers between devices  7.67 us (5%)
  matrix products  6.98 us (4%)
  other arithmetic  2.34 us (1%)
  blocking collectives  1.98 us (1%)
    reduce_scatter x1, waiting for transfers between devices, local(): lax.psum_scatter(corner_term, 'wide', scatter_dimension=0, tiled=True)  62.5 us
    all_gather x1, waiting for transfers between devices, local(): lax.all_gather(factor_panel, 'wide', axis=0, tiled=True)  38.2 us
    unnamed x28, local copies, waits for them, and re-layouts  12 us
    all_to_all x1, starting transfers between devices, local(): lax.all_to_all(jnp.stack(jnp.split(panel_cols, lax.axis_size(('wide', 'na...  7.55 us
    all_to_all x1, waiting for transfers between devices, local(): lax.all_to_all(jnp.stack(jnp.split(panel_cols, lax.axis_size(('wide', 'na...  6.22 us
    dot_general x1, matrix products, local(): jnp.dot(inverse_flat, lax.all_gather(factor_panel, 'wide', axis=0, tiled=...  3.8 us
    reduce_scatter x1, waiting for transfers between devices, local(): lax.psum_scatter(partial_value, 'narrow', scatter_dimension=1, tiled=True)  3.75 us
  transfers between devices with their start and end apart: 4, of which 4 were waited for; matrix products, arithmetic and copies ran while one was open for 1% of the time, Pallas kernels for 0%

profile of v1, /device:TPU:0, one launch (start us, length us, event | category | flops | bytes accessed | tf_op | source)
XLA Modules:
  0.0 157.2 jit_solution(12368213506509311730)
XLA Ops:
  7.2 1.0 multiply_subtract_fusion
  8.2 0.6 constant_dynamic-update-slice_fusion.15
  8.8 0.0 copy-start
  8.8 0.6 constant_dynamic-update-slice_fusion.14
  9.4 0.6 constant_dynamic-update-slice_fusion.13
  10.0 0.6 constant_dynamic-update-slice_fusion.12
  10.6 0.6 constant_dynamic-update-slice_fusion.11
  11.2 0.6 constant_dynamic-update-slice_fusion.10
  11.8 0.6 constant_dynamic-update-slice_fusion.9
  12.4 0.6 constant_dynamic-update-slice_fusion.8
  13.0 0.6 constant_dynamic-update-slice_fusion.7
  13.6 0.6 constant_dynamic-update-slice_fusion.6
  14.2 0.6 constant_dynamic-update-slice_fusion.5
  14.8 0.6 constant_dynamic-update-slice_fusion.4
  15.4 0.6 constant_dynamic-update-slice_fusion.3
  16.0 0.6 constant_dynamic-update-slice_fusion.2
  16.6 0.6 constant_dynamic-update-slice_fusion.1
  17.2 0.6 constant_dynamic-update-slice_fusion
  17.8 0.0 copy-start.4
  17.8 7.5 %all-to-all-start = ((f32[16,16,128]{2,1,0:T(8,128)}), f32[16,16,128]{2,1,0:T(8,128)S(1)}, u32[]{:S(2)}, u32[]{:S(2)}) async-start(f32[16,16,128]{2,1,0:T(8,128)} %constant_dynamic-update-slice_fusion), calls=%async_computation | async-start | bytes 262144 | tf_op jit(solution)/shard_map/all_to_all | solution.py:13
  25.3 0.0 copy-start.5
  25.3 0.0 all-gather.2.cloned.1.call-start
  25.4 0.0 copy-done.4
  25.4 0.6 copy-done.5
  26.0 0.0 copy-done
  26.0 0.0 copy-start.2
  26.0 1.0 gather_fusion
  27.0 6.2 %all-to-all-done = f32[16,16,128]{2,1,0:T(8,128)S(1)} async-done(((f32[16,16,128]{2,1,0:T(8,128)}), f32[16,16,128]{2,1,0:T(8,128)S(1)}, u32[]{:S(2)}, u32[]{:S(2)}) %all-to-all-start) | async-done | bytes 131104 | tf_op jit(solution)/shard_map/all_to_all | solution.py:13
  33.2 0.1 copy.8
  33.3 1.0 convolution_multiply_fusion
  34.3 0.0 all-gather.2.cloned.1.call-update
  34.4 0.0 reduce-scatter.3.cloned.1.call-start
  34.4 38.2 %all-gather.2.cloned.1.call-done = f32[1024,256]{1,0:T(8,128)} async-done(((f32[128,256]{1,0:T(8,128)}), f32[1024,256]{1,0:T(8,128)}) %all-gather.2.cloned.1.call-update) | async-done | bytes 1048592 | tf_op jit(solution)/shard_map/all_gather | solution.py:37
  72.6 0.0 copy-done.2
  72.6 3.8 %convolution_bitcast_fusion = f32[256,256]{0,1:T(8,128)} fusion(f32[1024,256]{1,0:T(8,128)} %all-gather.2.cloned.1.call-done, f32[32,8,8,128]{3,2,1,0:T(8,128)S(1)} %bitcast.85), kind=kOutput, calls=%fused_computation.1 | convolution fusion | flops 805306368 | bytes 2359296 | tf_op jit(solution)/shard_map/dot_general | solution.py:35
  76.4 0.0 copy-start.1
  76.4 0.0 reduce-scatter.3.cloned.1.call-update
  76.4 0.0 reduce-scatter.5.cloned.1.call-start
  76.4 0.8 copy-done.1
  77.3 2.0 %all_gather.7 = f32[256,256]{1,0:T(8,128)S(1)} all-gather(f32[128,256]{1,0:T(8,128)S(1)} %bitcast.84), channel_id=1, replica_groups=mesh['pole'=2,'wide'=8,'narrow'=2] {'narrow'}, dimensions={0}, use_global_device_ids=true | all-gather | bytes 393216 | tf_op jit(solution)/shard_map/all_gather | solution.py:42
  79.3 3.7 %reduce-scatter.3.cloned.1.call-done = f32[256,128]{0,1:T(8,128)} async-done(((f32[256,256]{0,1:T(8,128)}), f32[256,128]{0,1:T(8,128)}) %reduce-scatter.3.cloned.1.call-update) | async-done | bytes 131088 | tf_op jit(solution)/shard_map/reduce_scatter | solution.py:41
  83.0 2.2 %fusion.7 = f32[256,128]{1,0:T(8,128)} fusion(f32[256,256]{1,0:T(8,128)S(1)} %all_gather.7, f32[256,128]{0,1:T(8,128)} %reduce-scatter.3.cloned.1.call-done), kind=kOutput, calls=%fused_computation.48 | convolution fusion | flops 100696064 | bytes 524288 | tf_op jit(solution)/shard_map/dot_general | solution.py:43
  85.2 0.0 copy-start.3
  85.2 0.0 reduce-scatter.5.cloned.1.call-update
  85.2 0.9 copy-done.3
  86.1 0.8 copy.9
  86.8 62.5 %reduce-scatter.5.cloned.1.call-done = f32[32,128]{1,0:T(8,128)} async-done(((f32[256,128]{1,0:T(8,128)}), f32[32,128]{1,0:T(8,128)}) %reduce-scatter.5.cloned.1.call-update) | async-done | bytes 16400 | tf_op jit(solution)/shard_map/reduce_scatter | solution.py:50
  149.4 1.3 dynamic-slice_subtract_fusion
  (5 shorter events, 0.0 us)
Async XLA Ops:
  8.8 17.2 %copy-start = (f32[256,256]{1,0:T(8,128)S(1)}, f32[256,256]{1,0:T(8,128)}, u32[]{:S(2)}) copy-start(f32[256,256]{1,0:T(8,128)} %param.10) | copy-start | bytes 786436
  17.8 7.6 %copy-start.4 = (s32[256]{0:T(256)S(1)}, s32[256]{0:T(256)}, u32[]{:S(2)}) copy-start(s32[256]{0:T(256)} %param.8) | copy-start | bytes 3076
  17.8 15.5 %all-to-all-start = ((f32[16,16,128]{2,1,0:T(8,128)}), f32[16,16,128]{2,1,0:T(8,128)S(1)}, u32[]{:S(2)}, u32[]{:S(2)}) async-start(f32[16,16,128]{2,1,0:T(8,128)} %constant_dynamic-update-slice_fusion), calls=%async_computation | async-start | bytes 262144 | tf_op jit(solution)/shard_map/all_to_all | solution.py:13
  25.3 0.7 copy-start.5
  25.3 47.2 %all-gather.2.cloned.1.call-start = ((), (), s32[]{:S(2)}) async-start(), calls=%async_computation.3 | async-start | bytes 1179648 | tf_op jit(solution)/shard_map/all_gather | solution.py:37
  26.0 46.6 %copy-start.2 = (f32[256,8,1,128]{3,2,1,0:T(1,128)S(1)}, f32[256,8,1,128]{3,2,1,0:T(1,128)}, u32[]{:S(2)}) copy-start(f32[256,8,1,128]{3,2,1,0:T(1,128)} %param.11) | copy-start | bytes 3145732
  34.4 48.6 %reduce-scatter.3.cloned.1.call-start = ((), (), s32[]{:S(2)}) async-start(), calls=%async_computation.4 | async-start | bytes 393216 | tf_op jit(solution)/shard_map/reduce_scatter | solution.py:41
  76.4 0.9 copy-start.1
  76.4 73.0 %reduce-scatter.5.cloned.1.call-start = ((), (), s32[]{:S(2)}) async-start(), calls=%async_computation.5 | async-start | bytes 147456 | tf_op jit(solution)/shard_map/reduce_scatter | solution.py:50
  85.2 0.9 copy-start.3
Sparse Core Ops, SparseCore 0:
  34.5 38.0 all-gather.1
  76.5 6.4 reduce-scatter.2
  86.3 62.9 reduce-scatter.4

commit v2 on v0

--- a/solution.py
+++ b/solution.py
@@ -28,7 +28,9 @@
     inverse_flat = ainv_cc.reshape(rows_here, -1)
     partial_value = jnp.dot(
         inverse_flat,
-        lax.all_gather(factor_panel, "wide", axis=0, tiled=True),
+        jnp.concatenate(
+            lax.all_to_all(jnp.stack([factor_panel] * lax.axis_size("wide")), "wide", 0, 0), axis=0
+        ),
         precision=lax.Precision.HIGHEST,
         preferred_element_type=jnp.float32,
     )

time: 149 us -> 138 us (0.926)
  waiting for transfers between devices: 111 us -> 73.6 us
  blocking collectives: 1.98 us -> 30.3 us
  matrix products: 6.98 us -> 5.09 us
    all_gather x1 -> x0, waiting for transfers between devices: 38.2 us -> none  [local(): lax.all_gather(factor_panel, 'wide', axis=0, tiled=True)]
    all_to_all x0 -> x1, blocking collectives: none -> 28.3 us  [local(): lax.all_to_all(jnp.stack([factor_panel] * lax.axis_size('wide')), 'wide',...]
    unnamed x13 -> x11, local copies, waits for them, and re-layouts: 3.05 us -> 2.22 us
  transfers between devices with their start and end apart: 4 -> 3, of which waited for: 4 -> 3; matrix products, arithmetic and copies ran while one was open for 1% -> 1% of each run, Pallas kernels for 0% -> 0%
where the time goes in v2:
time: 138 us; the launch traced here: 137 us
  waiting for transfers between devices  73.6 us (53%)
  blocking collectives  30.3 us (22%)
  between operations  14.1 us (10%)
  starting transfers between devices  7.63 us (6%)
  matrix products  5.09 us (4%)
  local copies, waits for them, and re-layouts  3.37 us (2%)
  other arithmetic  3.04 us (2%)
    reduce_scatter x1, waiting for transfers between devices, local(): lax.psum_scatter(corner_term, 'wide', scatter_dimension=0, tiled=True)  62.5 us
    all_to_all x1, blocking collectives, local(): lax.all_to_all(jnp.stack([factor_panel] * lax.axis_size('wide')), 'wide',...  28.3 us
    all_to_all x1, starting transfers between devices, local(): lax.all_to_all(panel_cols, ('wide', 'narrow'), split_axis=1, concat_axis=...  7.55 us
    all_to_all x1, waiting for transfers between devices, local(): lax.all_to_all(panel_cols, ('wide', 'narrow'), split_axis=1, concat_axis=...  6.24 us
    reduce_scatter x1, waiting for transfers between devices, local(): lax.psum_scatter(partial_value, 'narrow', scatter_dimension=1, tiled=True)  4.84 us
  transfers between devices with their start and end apart: 3, of which 3 were waited for; matrix products, arithmetic and copies ran while one was open for 1% of the time, Pallas kernels for 0%

profile of v2, /device:TPU:0, one launch (start us, length us, event | category | flops | bytes accessed | tf_op | source)
XLA Modules:
  0.0 137.2 jit_solution(650887902012885658)
XLA Ops:
  7.2 0.0 copy-start
  7.2 1.7 %copy_bitcast_fusion = f32[16,16,128]{2,0,1:T(8,128)} fusion(f32[16,2048]{1,0:T(8,128)} %param.6, f32[16,2048]{1,0:T(8,128)} %param.7), kind=kLoop, calls=%fused_computation.7 | loop fusion | flops 65536 | bytes 393216 | tf_op jit(solution)/shard_map/all_to_all | solution.py:12
  8.9 0.0 copy-start.3
  8.9 7.5 %all-to-all-start = ((f32[16,16,128]{2,0,1:T(8,128)}), f32[16,16,128]{2,0,1:T(8,128)S(1)}, u32[]{:S(2)}, u32[]{:S(2)}) async-start(f32[16,16,128]{2,0,1:T(8,128)} %copy_bitcast_fusion), calls=%async_computation | async-start | bytes 262144 | tf_op jit(solution)/shard_map/all_to_all | solution.py:12
  16.4 0.0 copy-start.4
  16.4 0.0 reduce-scatter.3.cloned.1.call-start
  16.5 0.0 copy-done.3
  16.5 0.6 copy-done.4
  17.1 0.0 copy-done
  17.1 1.0 gather_fusion
  18.1 6.2 %all-to-all-done = f32[16,16,128]{2,0,1:T(8,128)S(1)} async-done(((f32[16,16,128]{2,0,1:T(8,128)}), f32[16,16,128]{2,0,1:T(8,128)S(1)}, u32[]{:S(2)}, u32[]{:S(2)}) %all-to-all-start) | async-done | bytes 131104 | tf_op jit(solution)/shard_map/all_to_all | solution.py:12
  24.3 0.1 copy.16
  24.4 0.4 convolution_multiply_fusion
  24.8 0.1 stack.3
  24.9 0.0 copy-start.1
  24.9 28.3 %all_to_all.24 = f32[8,128,256]{2,1,0:T(8,128)S(1)} all-to-all(f32[8,128,256]{2,1,0:T(8,128)S(1)} %stack.3), channel_id=1, replica_groups=mesh['pole'=2,'wide'=8,'narrow'=2] {'wide'}, dimensions={0} | all-to-all | bytes 2097152 | tf_op jit(solution)/shard_map/all_to_all | solution.py:32
  53.2 0.0 copy-done.1
  53.2 2.6 %convolution_bitcast_fusion = f32[256,256]{0,1:T(8,128)} fusion(f32[1024,256]{1,0:T(8,128)S(1)} %bitcast.27, f32[32,8,8,128]{3,2,1,0:T(8,128)S(1)} %bitcast.30), kind=kOutput, calls=%fused_computation.1 | convolution fusion | flops 805306368 | bytes 2359296 | tf_op jit(solution)/shard_map/dot_general | solution.py:29
  55.8 0.0 reduce-scatter.3.cloned.1.call-update
  55.8 0.0 reduce-scatter.5.cloned.1.call-start
  55.9 2.0 %all_gather.3 = f32[256,256]{1,0:T(8,128)S(1)} all-gather(f32[128,256]{1,0:T(8,128)S(1)} %bitcast.29), channel_id=1, replica_groups=mesh['pole'=2,'wide'=8,'narrow'=2] {'narrow'}, dimensions={0}, use_global_device_ids=true | all-gather | bytes 393216 | tf_op jit(solution)/shard_map/all_gather | solution.py:38
  57.9 4.8 %reduce-scatter.3.cloned.1.call-done = f32[256,128]{0,1:T(8,128)} async-done(((f32[256,256]{0,1:T(8,128)}), f32[256,128]{0,1:T(8,128)}) %reduce-scatter.3.cloned.1.call-update) | async-done | bytes 131088 | tf_op jit(solution)/shard_map/reduce_scatter | solution.py:37
  62.7 2.1 %fusion.7 = f32[256,128]{1,0:T(8,128)} fusion(f32[256,256]{1,0:T(8,128)S(1)} %all_gather.3, f32[256,128]{0,1:T(8,128)} %reduce-scatter.3.cloned.1.call-done), kind=kOutput, calls=%fused_computation.17 | convolution fusion | flops 100696064 | bytes 524288 | tf_op jit(solution)/shard_map/dot_general | solution.py:39
  64.9 0.0 copy-start.2
  64.9 0.0 reduce-scatter.5.cloned.1.call-update
  64.9 0.9 copy-done.2
  65.8 0.8 copy.17
  66.5 62.5 %reduce-scatter.5.cloned.1.call-done = f32[32,128]{1,0:T(8,128)} async-done(((f32[256,128]{1,0:T(8,128)}), f32[32,128]{1,0:T(8,128)}) %reduce-scatter.5.cloned.1.call-update) | async-done | bytes 16400 | tf_op jit(solution)/shard_map/reduce_scatter | solution.py:46
  129.0 1.3 dynamic-slice_subtract_fusion
  (5 shorter events, 0.0 us)
Async XLA Ops:
  7.2 9.9 %copy-start = (f32[256,256]{1,0:T(8,128)S(1)}, f32[256,256]{1,0:T(8,128)}, u32[]{:S(2)}) copy-start(f32[256,256]{1,0:T(8,128)} %param.10) | copy-start | bytes 786436
  8.9 7.6 %copy-start.3 = (s32[256]{0:T(256)S(1)}, s32[256]{0:T(256)}, u32[]{:S(2)}) copy-start(s32[256]{0:T(256)} %param.8) | copy-start | bytes 3076
  8.9 15.5 %all-to-all-start = ((f32[16,16,128]{2,0,1:T(8,128)}), f32[16,16,128]{2,0,1:T(8,128)S(1)}, u32[]{:S(2)}, u32[]{:S(2)}) async-start(f32[16,16,128]{2,0,1:T(8,128)} %copy_bitcast_fusion), calls=%async_computation | async-start | bytes 262144 | tf_op jit(solution)/shard_map/all_to_all | solution.py:12
  16.4 0.7 copy-start.4
  16.4 46.3 %reduce-scatter.3.cloned.1.call-start = ((), (), s32[]{:S(2)}) async-start(), calls=%async_computation.4 | async-start | bytes 393216 | tf_op jit(solution)/shard_map/reduce_scatter | solution.py:37
  24.9 28.3 %copy-start.1 = (f32[256,8,1,128]{3,2,1,0:T(1,128)S(1)}, f32[256,8,1,128]{3,2,1,0:T(1,128)}, u32[]{:S(2)}) copy-start(f32[256,8,1,128]{3,2,1,0:T(1,128)} %param.11) | copy-start | bytes 3145732
  55.8 73.2 %reduce-scatter.5.cloned.1.call-start = ((), (), s32[]{:S(2)}) async-start(), calls=%async_computation.5 | async-start | bytes 147456 | tf_op jit(solution)/shard_map/reduce_scatter | solution.py:46
  64.9 0.9 copy-start.2
Sparse Core Ops, SparseCore 0:
  55.9 6.7 reduce-scatter.2
  66.0 62.9 reduce-scatter.4
